TPU v7x, 32 devices: a whole 2x2x4 slice. The times are simulated.
32 devices in a mesh: section: 4 (over x, core), gx: 2 (over y), gy: 4 (over z).
Axes of the slice: x: 2, y: 2, z: 4, core: 2. Of those that a mesh axis runs over, the one named last changes fastest.
Arguments:
- voltage: float32 [8, 64, 1024], P(None, ('section', 'gx'), 'gy'), may hold values from -1.8 to 1.8
- capacity: float32 [8, 64, 1024], P(None, ('section', 'gx'), 'gy'), may hold values from 0.05 to 0.5
- node_class: int32 [8, 64, 1024], P(None, ('section', 'gx'), 'gy'), may hold values from 0 to 7
- via_sites: int32 [7, 64, 1024], P(None, ('section', 'gx'), 'gy'), may hold values 0 or 1
- ball_sites: int32 [64, 1024], P(('section', 'gx'), 'gy'), may hold values 0 or 1
- load_type: int32 [64, 1024], P(('section', 'gx'), 'gy'), may hold values from 0 to 15
- load_table: float32 [16, 5], replicated, may hold values from -4 to 4
Outputs:
- sections: float32 [5, 8, 64, 1024], P(None, None, ('section', 'gx'), 'gy')
- next_voltage: float32 [8, 64, 1024], P(None, ('section', 'gx'), 'gy')
Inputs may be any that keep to these rules, and one draw needn't show every extreme that they name: `node_class`: index into the table of 8 conductances. `load_type`: row of load_table.
All inputs are finite; a program needn't handle non-finite values. No bound on the sum of `via_sites` or of `ball_sites` on one device may be relied on, other than what follows from the above.
Results may differ from a plain program's by a relative error of at most 0.0003.
Values sent between devices are 32-bit elements; how exact they have to be, the bound alone decides.
A program may use at most 128 MiB of HBM per device.

v0:
```python
import functools

import jax
import jax.numpy as jnp
from jax import lax
from jax.experimental import pallas as pl
from jax.experimental.pallas import tpu as pltpu
from jax.sharding import PartitionSpec as P

SECTIONS = 5
LEVELS = 3
LOADS = 16
LANES = 128
ONE_CYCLE = 28
BOTH_CYCLES = 56

node_table = (0.35, 0.55, 0.8, 1.1, 1.5, 2.0, 2.7, 3.6)
via_conductance = 2.5
ball_conductance = 4.0
damping = 0.8
slab_partner = (0, 2, 1, 4, 3)
row_axes = ("section", "gx")


def pair_times(first, second):
    return (
        first[0] * second[0] - first[1] * second[1],
        first[0] * second[1] + first[1] * second[0],
    )


def pair_over(first, second):
    divisor = second[0] * second[0] + second[1] * second[1]
    return (
        (first[0] * second[0] + first[1] * second[1]) / divisor,
        (first[1] * second[0] - first[0] * second[1]) / divisor,
    )


def pair_minus(first, second):
    return (first[0] - second[0], first[1] - second[1])


def poly_value(coeffs, point):
    total = (0.0, 0.0)
    for c in reversed(coeffs):
        total = pair_times(total, point)
        total = (total[0] + c, total[1])
    return total


def poly_product(first, second):
    result = [0.0] * (len(first) + len(second) - 1)
    for i in range(len(first)):
        for j in range(len(second)):
            result[i + j] = result[i + j] + first[i] * second[j]
    return result


def poly_roots(coeffs):
    leading = coeffs[-1]
    scaled = [c / leading for c in coeffs]
    degree = len(coeffs) - 1
    guesses = []
    current = (1.0, 0.0)
    for k in range(degree):
        guesses.append(current)
        current = pair_times(current, (0.4, 0.9))
    for repeat_index in range(800):
        for k in range(degree):
            divisor = (1.0, 0.0)
            for j in range(degree):
                if j != k:
                    divisor = pair_times(divisor, pair_minus(guesses[k], guesses[j]))
            guesses[k] = pair_minus(guesses[k], pair_over(poly_value(scaled, guesses[k]), divisor))
    return guesses


def matrix_product(first, second):
    return [
        [
            sum((first[i][k] * second[k][j] for k in range(len(second))))
            for j in range(len(second[0]))
        ]
        for i in range(len(first))
    ]


def matrix_inverse(matrix):
    order = len(matrix)
    work = [list(matrix[i]) + [1.0 if i == j else 0.0 for j in range(order)] for i in range(order)]
    for column in range(order):
        pivot = column
        for i in range(column + 1, order):
            if abs(work[i][column]) > abs(work[pivot][column]):
                pivot = i
        work[column], work[pivot] = (work[pivot], work[column])
        factor = work[column][column]
        work[column] = [entry / factor for entry in work[column]]
        for i in range(order):
            if i != column:
                scale_row = work[i][column]
                work[i] = [work[i][j] - scale_row * work[column][j] for j in range(2 * order)]
    return [row[order:] for row in work]


def eigen_vector(matrix, value):
    order = len(matrix)
    size_inner = order - 1
    system = []
    for i in range(size_inner):
        row = []
        for j in range(order):
            entry = (matrix[i][j], 0.0)
            if i == j:
                entry = pair_minus(entry, value)
            row.append(entry)
        row[order - 1] = (-row[order - 1][0], -row[order - 1][1])
        system.append(row)
    for column in range(size_inner):
        pivot = column
        for i in range(column + 1, size_inner):
            left_size = system[i][column][0] ** 2 + system[i][column][1] ** 2
            right_size = system[pivot][column][0] ** 2 + system[pivot][column][1] ** 2
            if left_size > right_size:
                pivot = i
        system[column], system[pivot] = (system[pivot], system[column])
        for i in range(size_inner):
            if i != column:
                factor = pair_over(system[i][column], system[column][column])
                system[i] = [
                    pair_minus(system[i][j], pair_times(factor, system[column][j]))
                    for j in range(order)
                ]
    vector = [pair_over(system[i][order - 1], system[i][i]) for i in range(size_inner)]
    vector.append((1.0, 0.0))
    return vector


def radau_tables():
    section_count = 5
    generator = [1.0]
    for k in range(section_count - 1):
        generator = poly_product(generator, [0.0, 1.0])
    for k in range(section_count):
        generator = poly_product(generator, [-1.0, 1.0])
    for k in range(section_count - 1):
        generator = [j * generator[j] for j in range(1, len(generator))]
    abscissae = sorted((root[0] for root in poly_roots(generator)))
    vander = [[abscissae[i] ** j for j in range(section_count)] for i in range(section_count)]
    integrals = [
        [abscissae[i] ** (j + 1) / (j + 1) for j in range(section_count)]
        for i in range(section_count)
    ]
    butcher = matrix_product(integrals, matrix_inverse(vander))
    inverse = matrix_inverse(butcher)
    coeffs = [0.0] * (section_count + 1)
    coeffs[section_count] = 1.0
    current = [[0.0] * section_count for _ in range(section_count)]
    for k in range(1, section_count + 1):
        current = matrix_product(inverse, current)
        for i in range(section_count):
            current[i][i] = current[i][i] + coeffs[section_count - k + 1]
        applied = matrix_product(inverse, current)
        coeffs[section_count - k] = -sum((applied[i][i] for i in range(section_count))) / k
    eigen_values = poly_roots(coeffs)
    real_pick = 0
    for k in range(section_count):
        if abs(eigen_values[k][1]) < abs(eigen_values[real_pick][1]):
            real_pick = k
    upper_half = [k for k in range(section_count) if eigen_values[k][1] > 1e-09]
    upper_half = sorted(upper_half, key=lambda k: -eigen_values[k][0])
    columns = [[entry[0] for entry in eigen_vector(inverse, (eigen_values[real_pick][0], 0.0))]]
    for k in upper_half:
        vector = eigen_vector(inverse, eigen_values[k])
        columns.append([entry[0] for entry in vector])
        columns.append([entry[1] for entry in vector])
    transform = [[columns[j][i] for j in range(section_count)] for i in range(section_count)]
    inverse_transform = matrix_inverse(transform)
    blocks = matrix_product(matrix_product(inverse_transform, inverse), transform)
    diagonal = [blocks[k][k] for k in range(section_count)]
    coupling = [
        blocks[k][slab_partner[k]] if slab_partner[k] != k else 0.0 for k in range(section_count)
    ]
    return (transform, inverse_transform, diagonal, coupling)


def lookup(classes, values_table):
    result = jnp.zeros(classes.shape, jnp.float32)
    for k in range(len(values_table)):
        result = result + jnp.where(classes == k, jnp.float32(values_table[k]), jnp.float32(0.0))
    return result


def series(near_side, far_side):
    return 2.0 * near_side * far_side / (near_side + far_side)


def left_by(value, count):
    return pltpu.roll(value, LANES - count, axis=1)


def right_by(value, count):
    return pltpu.roll(value, count, axis=1)


def from_above(value):
    return pltpu.roll(value, value.shape[0] - 1, axis=0)


def from_below(value):
    return pltpu.roll(value, 1, axis=0)


def lane_ids(layers):
    return lax.broadcasted_iota(jnp.int32, (layers, LANES), 1)


def layer_ids(layers):
    return lax.broadcasted_iota(jnp.int32, (layers, LANES), 0)


def flux(here, ahead, behind_flux, gx, gy, gv, stride):
    along_x = gx * (ahead - here)
    along_y = gy * (left_by(here, stride) - here)
    along_z = gv * (from_above(here) - here)
    total = (
        (along_x - behind_flux)
        + (along_y - right_by(along_y, stride))
        + (along_z - from_below(along_z))
    )
    return along_x, total


def group_lanes(value, stride, low_half):
    return value + jnp.where(low_half, left_by(value, stride), right_by(value, stride))


def weights(cap, total, lam0, alpha, beta):
    real = lam0 * cap + total
    mate = beta * cap
    both = alpha * cap + total
    scale = damping / (both * both + mate * mate)
    return damping / real, both * scale, mate * scale


def correct(residual, sw0, sw, mw):
    return (
        sw0 * residual[0],
        sw * residual[1] - mw * residual[2],
        sw * residual[2] + mw * residual[1],
    )


def sweep(level, refs, scal, add=None, coarse=None):
    lam0, alpha, beta = scal
    g, x_ref, f_ref = refs[level]
    rows = g.shape[1]
    layers = g.shape[2]
    stride = 2**level
    step = min(4, rows)
    zero = jnp.zeros((layers, LANES), jnp.float32)

    def value(k, base, half, r):
        loaded = x_ref[k, base + r]
        if add is not None:
            loaded = loaded + add[k, half + r // 2]
        return loaded

    def body(b, carry):
        behind = list(carry[:3])
        xs = [[carry[3 + k]] for k in range(3)]
        base = b * step
        half = b * (step // 2)
        for k in range(3):
            for r in range(1, step + 1):
                xs[k].append(value(k, base, half, r))
        results = []
        for r in range(step):
            i = base + r
            gx, gy, gv = g[0, i], g[1, i], g[2, i]
            ground, cap = g[3, i], g[4, i]
            local = (lam0 * cap + ground, alpha * cap + ground)
            mate = beta * cap
            x0, x1, x2 = xs[0][r], xs[1][r], xs[2][r]
            pulled = []
            for k in range(3):
                behind[k], total = flux(xs[k][r], xs[k][r + 1], behind[k], gx, gy, gv, stride)
                pulled.append(total)
            residual = (
                f_ref[0, i] - local[0] * x0 + pulled[0],
                f_ref[1, i] - local[1] * x1 - mate * x2 + pulled[1],
                f_ref[2, i] - local[1] * x2 + mate * x1 + pulled[2],
            )
            if coarse is None:
                change = correct(residual, g[5, i], g[6, i], g[7, i])
                results.append([xs[k][r] + change[k] for k in range(3)])
            else:
                results.append(residual)
        if coarse is None:
            for r in range(step):
                for k in range(3):
                    x_ref[k, base + r] = results[r][k]
        else:
            g_next, x_next, f_next = refs[level + 1]
            low_half = (lane_ids(layers) // stride) % 2 == 0
            for r in range(0, step, 2):
                i = half + r // 2
                summed = [
                    group_lanes(results[r][k] + results[r + 1][k], stride, low_half)
                    for k in range(3)
                ]
                first = correct(summed, g_next[5, i], g_next[6, i], g_next[7, i])
                for k in range(3):
                    f_next[k, i] = summed[k]
                    x_next[k, i] = first[k]
        return tuple(behind) + tuple(xs[k][step] for k in range(3))

    init = (zero,) * 3 + tuple(value(k, 0, 0, 0) for k in range(3))
    lax.fori_loop(0, rows // step, body, init)


def coarsen(level, refs, scal):
    g = refs[level][0]
    g_next = refs[level + 1][0]
    layers = g.shape[2]
    stride = 2**level
    rows = g_next.shape[1]
    step = min(4, rows)

    def body(b, behind):
        low_half = (lane_ids(layers) // stride) % 2 == 0
        for r in range(step):
            i = b * step + r
            j = 2 * b * step + 2 * r
            gx = group_lanes(g[0, j + 1], stride, low_half)
            crossing = g[1, j] + g[1, j + 1]
            gy = jnp.where(low_half, left_by(crossing, stride), crossing)
            gv = group_lanes(g[2, j] + g[2, j + 1], stride, low_half)
            ground = group_lanes(g[3, j] + g[3, j + 1], stride, low_half)
            cap = group_lanes(g[4, j] + g[4, j + 1], stride, low_half)
            total = gx + behind + gy + right_by(gy, 2 * stride) + gv + from_below(gv) + ground
            found = weights(cap, total, *scal)
            for k, entry in enumerate((gx, gy, gv, ground, cap) + found):
                g_next[k, i] = entry
            behind = gx
        return behind

    lax.fori_loop(0, rows // step, body, jnp.zeros((layers, LANES), jnp.float32))


def cycle(refs, scal):
    sweep(0, refs, scal)
    sweep(0, refs, scal, coarse=True)
    sweep(1, refs, scal)
    sweep(1, refs, scal, coarse=True)
    for _ in range(3):
        sweep(2, refs, scal)
    sweep(1, refs, scal, add=refs[2][1])
    sweep(1, refs, scal)
    sweep(0, refs, scal, add=refs[1][1])
    sweep(0, refs, scal)


def kernel(
    sizes, transform, params, send, voltage, sections, next_voltage,
    recv, surf, g0, g1, g2, x0, x1, x2, f0, f1, f2, packed, landed, out_buf, out_recv,
    send_sem, recv_sem, ring_send, ring_recv, out_send, out_recv_sem, own_sem,
):
    parts, gx_count, gy_count, width, margin, columns = sizes
    layers = voltage.shape[0]
    block = voltage.shape[1]
    rows = parts * block
    regions = parts // 2
    mine = lax.axis_index("section") * gx_count + lax.axis_index("gx")
    gy_here = lax.axis_index("gy")
    system = mine % 2
    region = gy_here * regions + mine // 2
    all_regions = regions * gy_count

    def group_device(index):
        return {"section": index // gx_count, "gx": index % gx_count}

    def region_device(index):
        place = (index % regions) * 2 + system
        return {
            "section": place // gx_count,
            "gx": place % gx_count,
            "gy": index // regions,
        }

    after = region_device((region + 1) % all_regions)
    before = region_device((region + all_regions - 1) % all_regions)

    barrier = pltpu.get_barrier_semaphore()
    for d in range(1, parts):
        pl.semaphore_signal(
            barrier,
            inc=1,
            device_id=group_device((mine + d) % parts),
            device_id_type=pl.DeviceIdType.MESH,
        )
    for place in (after, before):
        pl.semaphore_signal(
            barrier, inc=1, device_id=place, device_id_type=pl.DeviceIdType.MESH
        )
    pl.semaphore_wait(barrier, parts + 1)

    copies = []
    for d in range(1, parts):
        peer = (mine + d) % parts
        copy = pltpu.make_async_remote_copy(
            src_ref=send.at[peer // 2],
            dst_ref=recv.at[mine],
            send_sem=send_sem.at[d],
            recv_sem=recv_sem.at[d],
            device_id=group_device(peer),
            device_id_type=pl.DeviceIdType.MESH,
        )
        copy.start()
        copies.append(copy)
    own = pltpu.make_async_copy(send.at[mine // 2], recv.at[mine], own_sem)
    own.start()
    lam0, alpha, beta = params[0], params[1], params[2]
    shares = (params[3], params[4], params[5])
    scal = (lam0, alpha, beta)
    zero = jnp.zeros((layers, LANES), jnp.float32)
    for x_ref in (x0, x1, x2):
        for k in range(3):
            x_ref[k, x_ref.shape[1] - 1] = zero
    own.wait()
    for copy in copies:
        copy.wait()

    def loads(b, carry):
        kind = recv[b, 4 * block]
        sums = [zero, zero, zero]
        for t in range(LOADS):
            here = kind == float(t)
            for k in range(3):
                sums[k] = jnp.where(here, params[6 + 3 * t + k], sums[k])
        for k in range(3):
            surf[k, b] = sums[k]
        return carry

    lax.fori_loop(0, parts, loads, 0)

    lanes = lane_ids(layers)
    level_of = layer_ids(layers)
    column = region * width - margin + lanes
    inside = (column >= 0) & (column < columns)
    joined = inside & (column < columns - 1) & (lanes < LANES - 1)

    def fine(b, carry):
        behind_gx, behind_flux = carry
        following = jnp.minimum(b + 1, parts - 1)
        for r in range(block):
            i = b * block + r
            volt, cap = recv[b, 4 * r], recv[b, 4 * r + 1]
            conduct = jnp.where(inside, recv[b, 4 * r + 2], 1.0)
            sites = recv[b, 4 * r + 3]
            if r + 1 < block:
                volt_ahead, conduct_ahead = recv[b, 4 * r + 4], recv[b, 4 * r + 6]
            else:
                volt_ahead, conduct_ahead = recv[following, 0], recv[following, 2]
            conduct_ahead = jnp.where(inside, conduct_ahead, 1.0)
            gx = series(conduct, conduct_ahead)
            if r + 1 == block:
                gx = gx * (b < parts - 1).astype(jnp.float32)
            gy = jnp.where(joined, series(conduct, left_by(conduct, 1)), 0.0)
            gv = jnp.where(level_of < layers - 1, sites, 0.0)
            ground = jnp.where(level_of == 0, from_below(sites), 0.0)
            total = gx + behind_gx + gy + right_by(gy, 1) + gv + from_below(gv) + ground
            found = weights(cap, total, *scal)
            behind_flux, pulled = flux(volt, volt_ahead, behind_flux, gx, gy, gv, 1)
            leak = ground * volt - pulled
            for k, entry in enumerate((gx, gy, gv, ground, cap) + found):
                g0[k, i] = entry
            source = [
                jnp.where(
                    level_of == layers - 1,
                    jnp.broadcast_to(surf[k, b, r : r + 1, :], (layers, LANES)),
                    0.0,
                )
                - shares[k] * leak
                for k in range(3)
            ]
            first = correct(source, *found)
            for k in range(3):
                f0[k, i] = source[k]
                x0[k, i] = first[k]
            behind_gx = gx
        return behind_gx, behind_flux

    lax.fori_loop(0, parts, fine, (zero, zero))
    refs = ((g0, x0, f0), (g1, x1, f1), (g2, x2, f2))
    coarsen(0, refs, scal)
    coarsen(1, refs, scal)
    cycle(refs, scal)

    if margin < BOTH_CYCLES:
        share = LANES // margin
        groups = rows // share

        def pack(q, carry):
            for side, begin in ((0, width), (1, margin)):
                for k in range(3):
                    joint = zero
                    for t in range(share):
                        turn = (margin * t - begin) % LANES
                        moved = x0[k, q + groups * t]
                        if turn:
                            moved = right_by(moved, turn)
                        joint = jnp.where(lanes // margin == t, moved, joint)
                    packed[side, k, q] = joint
            return carry

        lax.fori_loop(0, groups, pack, 0)
        ring = []
        for side, place in ((0, after), (1, before)):
            copy = pltpu.make_async_remote_copy(
                src_ref=packed.at[side],
                dst_ref=landed.at[side],
                send_sem=ring_send.at[side],
                recv_sem=ring_recv.at[side],
                device_id=place,
                device_id_type=pl.DeviceIdType.MESH,
            )
            copy.start()
            ring.append(copy)
        for copy in ring:
            copy.wait()

        def unpack(q, carry):
            for k in range(3):
                low = landed[0, k, q]
                high = landed[1, k, q]
                for t in range(share):
                    turn_low = (-margin * t) % LANES
                    turn_high = (margin + width - margin * t) % LANES
                    a = right_by(low, turn_low) if turn_low else low
                    c = right_by(high, turn_high) if turn_high else high
                    x = x0[k, q + groups * t]
                    x = jnp.where(lanes < margin, a, jnp.where(lanes < margin + width, x, c))
                    x0[k, q + groups * t] = x
            return carry

        lax.fori_loop(0, groups, unpack, 0)

    sweep(0, refs, scal)
    cycle(refs, scal)

    share = LANES // width
    groups = block // share
    copies = []
    for d in range(parts):
        peer = (mine + d) % parts
        for k in range(3):
            for q in range(groups):
                joint = zero
                for t in range(share):
                    turn = (width * t - margin) % LANES
                    moved = x0[k, peer * block + q + groups * t]
                    if turn:
                        moved = right_by(moved, turn)
                    joint = jnp.where(lanes // width == t, moved, joint)
                out_buf[d, k * groups + q] = joint
        if d == 0:
            own = pltpu.make_async_copy(out_buf.at[0], out_recv.at[mine], own_sem)
            own.start()
            continue
        copy = pltpu.make_async_remote_copy(
            src_ref=out_buf.at[d],
            dst_ref=out_recv.at[mine],
            send_sem=out_send.at[d],
            recv_sem=out_recv_sem.at[d],
            device_id=group_device(peer),
            device_id_type=pl.DeviceIdType.MESH,
        )
        copy.start()
        copies.append(copy)
    own.wait()
    for copy in copies:
        copy.wait()

    for tile in range(regions // share):
        mixed = [[None] * block for _ in range(SECTIONS)]
        for q in range(groups):
            fields = []
            for n in range(share):
                first = 2 * (tile * share + n)
                fields.append(
                    [out_recv[first, k * groups + q] for k in range(3)]
                    + [out_recv[first + 1, k * groups + q] for k in (1, 2)]
                )
            for s in range(SECTIONS):
                sums = [
                    sum(transform[s][k] * fields[n][k] for k in range(SECTIONS))
                    for n in range(share)
                ]
                for t in range(share):
                    joint = zero
                    for n in range(share):
                        turn = (width * (n - t)) % LANES
                        moved = right_by(sums[n], turn) if turn else sums[n]
                        joint = jnp.where(lanes // width == n, moved, joint)
                    mixed[s][q + groups * t] = joint
        place = pl.ds(tile * LANES, LANES)
        for s in range(SECTIONS):
            turned = jnp.swapaxes(jnp.stack(mixed[s]), 0, 1)
            sections[s, :, :, place] = turned
            if s == SECTIONS - 1:
                next_voltage[:, :, place] = voltage[:, :, place] + turned


def local(voltage, capacity, node_class, via_sites, ball_sites, load_type, load_table):
    transform, inverse_transform, diagonal, coupling = radau_tables()
    layers, block, wide = voltage.shape
    gx_count = lax.axis_size("gx")
    gy_count = lax.axis_size("gy")
    parts = lax.axis_size("section") * gx_count
    regions = parts // 2
    width = wide // regions
    margin = (LANES - width) // 2
    sizes = (parts, gx_count, gy_count, width, margin, wide * gy_count)
    rows = parts * block

    conduct = lookup(node_class, node_table)
    sites = jnp.concatenate(
        [
            jnp.where(via_sites == 1, jnp.float32(via_conductance), jnp.float32(0.0)),
            jnp.where(ball_sites == 1, jnp.float32(ball_conductance), jnp.float32(0.0))[None],
        ],
        axis=0,
    )
    planes = jnp.stack([voltage, capacity, conduct, sites]).transpose(2, 0, 1, 3)
    planes = planes.reshape(4 * block, layers, wide)
    planes = jnp.concatenate([planes, load_type.astype(jnp.float32)[None]], axis=0)
    forward = [(i, i + 1) for i in range(gy_count - 1)]
    backward = [(i + 1, i) for i in range(gy_count - 1)]
    low = lax.ppermute(planes[..., wide - margin :], "gy", forward)
    high = lax.ppermute(planes[..., :margin], "gy", backward)
    planes = jnp.concatenate([low, planes, high], axis=-1)
    send = jnp.stack([planes[..., width * k : width * k + LANES] for k in range(regions)])

    mine = lax.axis_index("section") * gx_count + lax.axis_index("gx")
    leading = mine % 2 == 0

    def chosen(table):
        first = [table[0], table[1], table[2]]
        second = [table[0], table[3], table[4]]
        return jnp.where(
            leading, jnp.asarray(first, jnp.float32), jnp.asarray(second, jnp.float32)
        )

    mixing = chosen(inverse_transform)
    shifts = chosen(diagonal)
    couple = chosen(coupling)
    currents = jnp.sum(load_table[:, None, :] * mixing[None], axis=-1)
    params = jnp.concatenate(
        [shifts[:2], couple[1:2], jnp.sum(mixing, axis=1), currents.reshape(-1)]
    )

    def vmem(*shape):
        return pltpu.VMEM(shape, jnp.float32)

    def levels(count, extra):
        return [vmem(count, rows // 2**m + extra, layers, LANES) for m in range(LEVELS)]

    mid = rows * margin // LANES if margin < BOTH_CYCLES else 1
    back = 3 * block * width // LANES
    return pl.pallas_call(
        functools.partial(kernel, sizes, transform),
        out_shape=(
            jax.ShapeDtypeStruct((SECTIONS, layers, block, wide), jnp.float32),
            jax.ShapeDtypeStruct((layers, block, wide), jnp.float32),
        ),
        in_specs=[
            pl.BlockSpec(memory_space=pltpu.SMEM),
            pl.BlockSpec(memory_space=pltpu.VMEM),
            pl.BlockSpec(memory_space=pltpu.VMEM),
        ],
        out_specs=(
            pl.BlockSpec(memory_space=pltpu.VMEM),
            pl.BlockSpec(memory_space=pltpu.VMEM),
        ),
        scratch_shapes=[
            vmem(parts, 4 * block + 1, layers, LANES),
            vmem(3, parts, block, LANES),
            *levels(8, 0),
            *levels(3, 1),
            *levels(3, 0),
            vmem(2, 3, mid, layers, LANES),
            vmem(2, 3, mid, layers, LANES),
            vmem(parts, back, layers, LANES),
            vmem(parts, back, layers, LANES),
            pltpu.SemaphoreType.DMA((parts,)),
            pltpu.SemaphoreType.DMA((parts,)),
            pltpu.SemaphoreType.DMA((2,)),
            pltpu.SemaphoreType.DMA((2,)),
            pltpu.SemaphoreType.DMA((parts,)),
            pltpu.SemaphoreType.DMA((parts,)),
            pltpu.SemaphoreType.DMA,
        ],
        compiler_params=pltpu.CompilerParams(
            collective_id=0, has_side_effects=True, vmem_limit_bytes=60 * 1024 * 1024
        ),
    )(params, send, voltage)


def solution(mesh):
    return jax.shard_map(
        local,
        mesh=mesh,
        in_specs=(
            P(None, row_axes, "gy"),
            P(None, row_axes, "gy"),
            P(None, row_axes, "gy"),
            P(None, row_axes, "gy"),
            P(row_axes, "gy"),
            P(row_axes, "gy"),
            P(),
        ),
        out_specs=(P(None, None, row_axes, "gy"), P(None, row_axes, "gy")),
        check_vma=False,
    )
```

profile of v0, /device:TPU:0, one launch (start us, length us, event | category | flops | bytes accessed | tf_op | source)
XLA Modules:
  0.0 96.3 jit_solution(186777169570678549)
XLA Ops:
  0.6 0.0 copy-start.4
  0.6 0.7 convert_bitcast_fusion
  1.3 0.0 copy-done.4
  1.3 0.0 copy-start.2
  1.4 0.9 compare_select_fusion
  2.2 0.0 copy-done.2
  2.2 0.0 copy-start
  2.2 0.0 copy-start.3
  2.2 0.1 maximum_bitcast_fusion.1
  2.3 0.8 copy-done
  3.1 0.0 copy-done.3
  3.1 0.1 copy.21
  3.2 0.1 fusion.2
  3.3 5.0 %collective-permute-start = (f32[33,8,32]{2,1,0:T(8,128)S(1)}, f32[33,8,32]{2,1,0:T(8,128)S(1)}, u32[]{:S(2)}, u32[]{:S(2)}) collective-permute-start(f32[33,8,32]{2,1,0:T(8,128)S(1)} %get-tuple-element.6), channel_id=1, source_target_pairs={{0,1},{1,2},{2,3},{4,5},{5,6},{6,7},{8,9},{9,10},{10,11},{12,13},{... | collective-permute-start | bytes 101384 | tf_op jit(solution)/shard_map/ppermute | solution.py:641
  8.3 1.3 %collective-permute-start.1 = (f32[33,8,32]{2,1,0:T(8,128)S(1)}, f32[33,8,32]{2,1,0:T(8,128)S(1)}, u32[]{:S(2)}, u32[]{:S(2)}) collective-permute-start(f32[33,8,32]{2,1,0:T(8,128)S(1)} %get-tuple-element.7), channel_id=1, source_target_pairs={{1,0},{2,1},{3,2},{5,4},{6,5},{7,6},{9,8},{10,9},{11,10},{13,12},{... | collective-permute-start | bytes 101384 | tf_op jit(solution)/shard_map/ppermute | solution.py:642
  9.6 0.0 copy-start.11
  9.6 0.0 copy-start.8
  9.6 0.0 copy-start.9
  9.6 0.0 copy-start.10
  9.7 0.6 copy-done.11
  10.3 0.0 copy-done.8
  10.3 0.0 copy-done.9
  10.3 0.0 copy-done.10
  10.3 0.0 copy-start.7
  10.3 0.0 copy-start.6
  10.3 0.6 slice.27
  10.9 0.1 copy-done.7
  11.0 0.0 copy-done.6
  11.0 0.1 fusion.7
  11.1 0.0 copy-start.5
  11.1 0.1 copy.19
  11.2 0.6 copy-done.5
  11.8 0.1 multiply_reduce_fusion
  11.9 0.1 copy.20
  12.0 0.1 reshape.12
  12.1 1.2 %pad_maximum_fusion.6.params = f32[54]{0:T(128)} fusion(f32[48]{0:T(128)S(1)} %reshape.12, f32[3]{0:T(128)S(1)} %get-tuple-element.8, f32[1]{0:T(128)} %slice.27, f32[2]{0:T(128)S(1)} %bitcast.26), kind=kLoop, calls=%fused_computation.30 | loop fusion | flops 162 | bytes 432 | tf_op jit(solution)/shard_map/concatenate | solution.py:660
  13.3 0.0 collective-permute-done
  13.3 1.9 %collective-permute-done.1 = f32[33,8,32]{2,1,0:T(8,128)S(1)} collective-permute-done((f32[33,8,32]{2,1,0:T(8,128)S(1)}, f32[33,8,32]{2,1,0:T(8,128)S(1)}, u32[]{:S(2)}, u32[]{:S(2)}) %collective-permute-start.1) | collective-permute-done | bytes 33824 | tf_op jit(solution)/shard_map/ppermute | solution.py:642
  15.2 0.2 fusion.6
  15.5 0.8 pad_maximum_fusion.send
  16.3 77.6 %shard_map.140 = (f32[5,8,8,256]{3,2,1,0:T(8,128)}, f32[8,8,256]{2,1,0:T(8,128)}) custom-call(f32[54]{0:T(128)} %pad_maximum_fusion.6.params, f32[4,33,8,128]{3,2,1,0:T(8,128)} %pad_maximum_fusion.send, f32[8,8,256]{2,1,0:T(8,128)} %voltage.1), custom_call_target="tpu_custom_call" | custom-call | tf_op jit(solution)/shard_map/pallas_call | solution.py:672
  93.9 0.0 copy-start.1
  93.9 1.8 %copy.24 = f32[5,8,8,256]{3,2,1,0:T(8,128)} copy(f32[5,8,8,256]{3,2,1,0:T(8,128)} %get-tuple-element.16) | data formatting | bytes 655360
  95.6 0.0 copy-done.1
  95.6 0.6 copy.25
  (3 shorter events, 0.0 us)
Async XLA Ops:
  0.6 0.7 copy-start.4
  1.3 0.9 copy-start.2
  2.2 0.8 copy-start
  2.2 0.9 copy-start.3
  3.3 10.0 %collective-permute-start = (f32[33,8,32]{2,1,0:T(8,128)S(1)}, f32[33,8,32]{2,1,0:T(8,128)S(1)}, u32[]{:S(2)}, u32[]{:S(2)}) collective-permute-start(f32[33,8,32]{2,1,0:T(8,128)S(1)} %get-tuple-element.6), channel_id=1, source_target_pairs={{0,1},{1,2},{2,3},{4,5},{5,6},{6,7},{8,9},{9,10},{10,11},{12,13},{... | collective-permute-start | bytes 101384 | tf_op jit(solution)/shard_map/ppermute | solution.py:641
  8.3 6.9 %collective-permute-start.1 = (f32[33,8,32]{2,1,0:T(8,128)S(1)}, f32[33,8,32]{2,1,0:T(8,128)S(1)}, u32[]{:S(2)}, u32[]{:S(2)}) collective-permute-start(f32[33,8,32]{2,1,0:T(8,128)S(1)} %get-tuple-element.7), channel_id=1, source_target_pairs={{1,0},{2,1},{3,2},{5,4},{6,5},{7,6},{9,8},{10,9},{11,10},{13,12},{... | collective-permute-start | bytes 101384 | tf_op jit(solution)/shard_map/ppermute | solution.py:642
  9.6 0.7 copy-start.11
  9.6 0.7 copy-start.8
  9.6 0.7 copy-start.9
  9.6 0.7 copy-start.10
  10.3 0.7 copy-start.7
  10.3 0.7 copy-start.6
  11.1 0.7 copy-start.5
  93.9 1.8 %copy-start.1 = (f32[8,8,256]{2,1,0:T(8,128)S(1)}, f32[8,8,256]{2,1,0:T(8,128)}, u32[]{:S(2)}) copy-start(f32[8,8,256]{2,1,0:T(8,128)} %get-tuple-element.17) | copy-start | bytes 196612
where the time goes:
time: 96.7 us; the launch traced here: 96.3 us
  Pallas kernels  77.6 us (80%)
  starting transfers between devices  6.26 us (6%)
  local copies, waits for them, and re-layouts  5.5 us (6%)
  other arithmetic  4.25 us (4%)
  waiting for transfers between devices  1.92 us (2%)
    pallas_call x1, Pallas kernels, local(): pl.pallas_call(functools.partial(kernel, sizes, transform), out_shape=(ja...  77.6 us
    ppermute x1, starting transfers between devices, local(): low = lax.ppermute(planes[..., wide - margin:], 'gy', forward)  4.96 us
    unnamed x26, local copies, waits for them, and re-layouts  4.56 us
  transfers between devices with their start and end apart: 2, of which 1 were waited for; matrix products, arithmetic and copies ran while one was open for 2% of the time, Pallas kernels for 0%

commit v1 on v0

--- a/solution.py
+++ b/solution.py
@@ -183,13 +183,6 @@
         blocks[k][slab_partner[k]] if slab_partner[k] != k else 0.0 for k in range(section_count)
     ]
     return (transform, inverse_transform, diagonal, coupling)
-
-
-def lookup(classes, values_table):
-    result = jnp.zeros(classes.shape, jnp.float32)
-    for k in range(len(values_table)):
-        result = result + jnp.where(classes == k, jnp.float32(values_table[k]), jnp.float32(0.0))
-    return result
 
 
 def series(near_side, far_side):
@@ -363,89 +356,215 @@
 
 
 def kernel(
-    sizes, transform, params, send, voltage, sections, next_voltage,
-    recv, surf, g0, g1, g2, x0, x1, x2, f0, f1, f2, packed, landed, out_buf, out_recv,
-    send_sem, recv_sem, ring_send, ring_recv, out_send, out_recv_sem, own_sem,
+    sizes, tables, load_table, voltage, capacity, node_class, via_sites, ball_sites, load_type,
+    sections, next_voltage,
+    planes, edge, edge_in, send, recv, surf, g0, g1, g2, x0, x1, x2, f0, f1, f2,
+    packed, landed, out_buf, out_recv,
+    edge_send, edge_recv, send_sem, recv_sem, pass_send, pass_recv,
+    ring_send, ring_recv, out_send, out_recv_sem, own_sem,
 ):
     parts, gx_count, gy_count, width, margin, columns = sizes
+    transform, inverse_transform, diagonal, coupling = tables
     layers = voltage.shape[0]
     block = voltage.shape[1]
-    rows = parts * block
+    wide = voltage.shape[2]
+    tiles = wide // LANES
     regions = parts // 2
-    mine = lax.axis_index("section") * gx_count + lax.axis_index("gx")
+    count = 4 * block + 1
+    section_here = lax.axis_index("section")
+    gx_here = lax.axis_index("gx")
     gy_here = lax.axis_index("gy")
-    system = mine % 2
-    region = gy_here * regions + mine // 2
+    mine = section_here * gx_count + gx_here
+    system = section_here % 2
     all_regions = regions * gy_count
+
+    def snake(place, row):
+        return place + (row % 2) * (gx_count - 1 - 2 * place)
+
+    def turned(place, column):
+        return place + (column % 2) * (regions - 1 - 2 * place)
+
+    pair = section_here // 2
+    spot = turned(pair * gx_count + snake(gx_here, pair), gy_here)
+    region = gy_here * regions + spot
+
+    def owner(place, column):
+        found = turned(place, column)
+        row = found // gx_count
+        return row * 2 + system, snake(found % gx_count, row)
 
     def group_device(index):
         return {"section": index // gx_count, "gx": index % gx_count}
 
     def region_device(index):
-        place = (index % regions) * 2 + system
-        return {
-            "section": place // gx_count,
-            "gx": place % gx_count,
-            "gy": index // regions,
-        }
+        column = index // regions
+        owner_section, owner_gx = owner(index % regions, column)
+        return {"section": owner_section, "gx": owner_gx, "gy": column}
 
     after = region_device((region + 1) % all_regions)
     before = region_device((region + all_regions - 1) % all_regions)
+    right = {"gy": (gy_here + 1) % gy_count}
+    left = {"gy": (gy_here + gy_count - 1) % gy_count}
+    partner = {"section": section_here + 1 - 2 * system}
 
     barrier = pltpu.get_barrier_semaphore()
-    for d in range(1, parts):
-        pl.semaphore_signal(
-            barrier,
-            inc=1,
-            device_id=group_device((mine + d) % parts),
-            device_id_type=pl.DeviceIdType.MESH,
-        )
-    for place in (after, before):
+    friends = [group_device((mine + d) % parts) for d in range(1, parts)]
+    friends += [after, before, right, left]
+    for place in friends:
         pl.semaphore_signal(
             barrier, inc=1, device_id=place, device_id_type=pl.DeviceIdType.MESH
         )
-    pl.semaphore_wait(barrier, parts + 1)
-
-    copies = []
-    for d in range(1, parts):
-        peer = (mine + d) % parts
-        copy = pltpu.make_async_remote_copy(
-            src_ref=send.at[peer // 2],
-            dst_ref=recv.at[mine],
-            send_sem=send_sem.at[d],
-            recv_sem=recv_sem.at[d],
-            device_id=group_device(peer),
+
+    def remote(source, target, source_sem, target_sem, place):
+        return pltpu.make_async_remote_copy(
+            src_ref=source,
+            dst_ref=target,
+            send_sem=source_sem,
+            recv_sem=target_sem,
+            device_id=place,
             device_id_type=pl.DeviceIdType.MESH,
         )
+
+    lanes = lane_ids(layers)
+    zero = jnp.zeros((layers, LANES), jnp.float32)
+
+    def turn_by(value, amount):
+        amount = amount % LANES
+        return right_by(value, amount) if amount else value
+
+    for tile in range(tiles):
+        place = pl.ds(tile * LANES, LANES)
+        kind = node_class[:, :, place]
+        conduct = jnp.full(kind.shape, node_table[0], jnp.float32)
+        for k in range(1, len(node_table)):
+            conduct = jnp.where(kind == k, jnp.float32(node_table[k]), conduct)
+        via = jnp.where(via_sites[:, :, place] == 1, jnp.float32(via_conductance), 0.0)
+        ball = jnp.where(ball_sites[:, place] == 1, jnp.float32(ball_conductance), 0.0)
+        sites = jnp.concatenate([via, ball[None]], axis=0)
+        for k, value in enumerate((voltage[:, :, place], capacity[:, :, place], conduct, sites)):
+            swapped = jnp.swapaxes(value, 0, 1)
+            for r in range(block):
+                planes[4 * r + k, :, place] = swapped[r]
+        planes[4 * block, :, place] = load_type[:, place].astype(jnp.float32)
+
+    share = LANES // margin
+    packs = edge.shape[1]
+    for side, begin in ((0, LANES - margin), (1, 0)):
+        place = pl.ds((tiles - 1) * LANES if side == 0 else 0, LANES)
+        for q in range(packs):
+            joint = zero
+            for t in range(share):
+                plane = q + packs * t
+                if plane < count:
+                    moved = turn_by(planes[plane, :, place], margin * t - begin)
+                    joint = jnp.where(lanes // margin == t, moved, joint)
+            edge[side, q] = joint
+    pl.semaphore_wait(barrier, parts + 3)
+    edges = [
+        remote(edge.at[i], edge_in.at[i], edge_send.at[i], edge_recv.at[i], place)
+        for i, place in ((0, right), (1, left))
+    ]
+    for copy in edges:
         copy.start()
-        copies.append(copy)
-    own = pltpu.make_async_copy(send.at[mine // 2], recv.at[mine], own_sem)
-    own.start()
-    lam0, alpha, beta = params[0], params[1], params[2]
-    shares = (params[3], params[4], params[5])
+
+    def build(k):
+        start = width * k - margin
+        for plane in range(count):
+            q, t = plane % packs, plane // packs
+            joint = None
+            for tile in range(-1, tiles + 1):
+                low = tile * LANES if tile >= 0 else -margin
+                high = (tile + 1) * LANES if tile >= 0 else 0
+                if tile == tiles:
+                    high = low + margin
+                if high <= start or low >= start + LANES:
+                    continue
+                if tile < 0:
+                    moved = turn_by(edge_in[0, q], -margin - start - margin * t)
+                elif tile == tiles:
+                    moved = turn_by(edge_in[1, q], wide - start - margin * t)
+                else:
+                    moved = turn_by(planes[plane, :, pl.ds(low, LANES)], low - start)
+                joint = moved if joint is None else jnp.where(lanes >= low - start, moved, joint)
+            send[k, plane] = joint
+
+    def direct(d, k):
+        owner_section, owner_gx = owner(k, gy_here)
+        return remote(
+            send.at[k], recv.at[mine], send_sem.at[d], recv_sem.at[d],
+            {"section": owner_section, "gx": owner_gx},
+        )
+
+    def handed(d, source, slot):
+        return remote(source, recv.at[slot], pass_send.at[d], pass_recv.at[d], partner)
+
+    own = pltpu.make_async_copy(send.at[spot], recv.at[mine], own_sem)
+
+    def dispatch(k):
+        d = (k - spot + regions) % regions
+
+        @pl.when(d != 0)
+        def _():
+            direct(d, k).start()
+
+        @pl.when(d == 0)
+        def _():
+            own.start()
+            handed(0, send.at[k], mine).start()
+
+    inner = [k for k in range(regions) if margin <= width * k <= wide - LANES + margin]
+    outer = [k for k in range(regions) if k not in inner]
+    for k in inner:
+        build(k)
+    for k in inner:
+        dispatch(k)
+    for copy in edges:
+        copy.wait()
+    for k in outer:
+        build(k)
+    for k in outer:
+        dispatch(k)
+
+    def pick(table):
+        return [
+            jnp.where(system == 0, jnp.float32(table[a]), jnp.float32(table[b]))
+            for a, b in ((0, 0), (1, 3), (2, 4))
+        ]
+
+    shifts = pick(diagonal)
+    lam0, alpha, beta = shifts[0], shifts[1], pick(coupling)[1]
+    shares = pick([sum(row) for row in inverse_transform])
+    mixing = [pick([row[j] for row in inverse_transform]) for j in range(SECTIONS)]
     scal = (lam0, alpha, beta)
-    zero = jnp.zeros((layers, LANES), jnp.float32)
     for x_ref in (x0, x1, x2):
         for k in range(3):
             x_ref[k, x_ref.shape[1] - 1] = zero
+    passes = [handed(0, send.at[spot], mine)]
+    for d in range(1, regions):
+        direct(d, (spot + d) % regions).wait()
+        owner_section, owner_gx = owner((spot - d + regions) % regions, gy_here)
+        slot = owner_section * gx_count + owner_gx
+        copy = handed(d, recv.at[slot], slot)
+        copy.start()
+        passes.append(copy)
     own.wait()
-    for copy in copies:
+    for copy in passes:
         copy.wait()
 
     def loads(b, carry):
         kind = recv[b, 4 * block]
-        sums = [zero, zero, zero]
+        currents = [zero] * SECTIONS
         for t in range(LOADS):
             here = kind == float(t)
-            for k in range(3):
-                sums[k] = jnp.where(here, params[6 + 3 * t + k], sums[k])
+            for j in range(SECTIONS):
+                currents[j] = jnp.where(here, load_table[t, j], currents[j])
         for k in range(3):
-            surf[k, b] = sums[k]
+            surf[k, b] = sum(mixing[j][k] * currents[j] for j in range(SECTIONS))
         return carry
 
     lax.fori_loop(0, parts, loads, 0)
 
-    lanes = lane_ids(layers)
+    rows = parts * block
     level_of = layer_ids(layers)
     column = region * width - margin + lanes
     inside = (column >= 0) & (column < columns)
@@ -552,26 +671,30 @@
 
     share = LANES // width
     groups = block // share
+    half = max(groups // 2, 1)
+    halves = groups // half
+    slot_out = spot * 2 + system
     copies = []
     for d in range(parts):
         peer = (mine + d) % parts
-        for k in range(3):
-            for q in range(groups):
-                joint = zero
-                for t in range(share):
-                    turn = (width * t - margin) % LANES
-                    moved = x0[k, peer * block + q + groups * t]
-                    if turn:
-                        moved = right_by(moved, turn)
-                    joint = jnp.where(lanes // width == t, moved, joint)
-                out_buf[d, k * groups + q] = joint
+        for index in range(half + 2 * groups):
+            k = 0 if index < half else 1 + (index - half) // groups
+            if k == 0:
+                q = index + (system * half if halves > 1 else 0)
+            else:
+                q = (index - half) % groups
+            joint = zero
+            for t in range(share):
+                moved = turn_by(x0[k, peer * block + q + groups * t], width * t - margin)
+                joint = jnp.where(lanes // width == t, moved, joint)
+            out_buf[d, index] = joint
         if d == 0:
-            own = pltpu.make_async_copy(out_buf.at[0], out_recv.at[mine], own_sem)
+            own = pltpu.make_async_copy(out_buf.at[0], out_recv.at[slot_out], own_sem)
             own.start()
             continue
         copy = pltpu.make_async_remote_copy(
             src_ref=out_buf.at[d],
-            dst_ref=out_recv.at[mine],
+            dst_ref=out_recv.at[slot_out],
             send_sem=out_send.at[d],
             recv_sem=out_recv_sem.at[d],
             device_id=group_device(peer),
@@ -590,8 +713,9 @@
             for n in range(share):
                 first = 2 * (tile * share + n)
                 fields.append(
-                    [out_recv[first, k * groups + q] for k in range(3)]
-                    + [out_recv[first + 1, k * groups + q] for k in (1, 2)]
+                    [out_recv[first + q // half, q % half]]
+                    + [out_recv[first, half + k * groups + q] for k in (0, 1)]
+                    + [out_recv[first + 1, half + k * groups + q] for k in (0, 1)]
                 )
             for s in range(SECTIONS):
                 sums = [
@@ -614,7 +738,6 @@
 
 
 def local(voltage, capacity, node_class, via_sites, ball_sites, load_type, load_table):
-    transform, inverse_transform, diagonal, coupling = radau_tables()
     layers, block, wide = voltage.shape
     gx_count = lax.axis_size("gx")
     gy_count = lax.axis_size("gy")
@@ -624,42 +747,8 @@
     margin = (LANES - width) // 2
     sizes = (parts, gx_count, gy_count, width, margin, wide * gy_count)
     rows = parts * block
-
-    conduct = lookup(node_class, node_table)
-    sites = jnp.concatenate(
-        [
-            jnp.where(via_sites == 1, jnp.float32(via_conductance), jnp.float32(0.0)),
-            jnp.where(ball_sites == 1, jnp.float32(ball_conductance), jnp.float32(0.0))[None],
-        ],
-        axis=0,
-    )
-    planes = jnp.stack([voltage, capacity, conduct, sites]).transpose(2, 0, 1, 3)
-    planes = planes.reshape(4 * block, layers, wide)
-    planes = jnp.concatenate([planes, load_type.astype(jnp.float32)[None]], axis=0)
-    forward = [(i, i + 1) for i in range(gy_count - 1)]
-    backward = [(i + 1, i) for i in range(gy_count - 1)]
-    low = lax.ppermute(planes[..., wide - margin :], "gy", forward)
-    high = lax.ppermute(planes[..., :margin], "gy", backward)
-    planes = jnp.concatenate([low, planes, high], axis=-1)
-    send = jnp.stack([planes[..., width * k : width * k + LANES] for k in range(regions)])
-
-    mine = lax.axis_index("section") * gx_count + lax.axis_index("gx")
-    leading = mine % 2 == 0
-
-    def chosen(table):
-        first = [table[0], table[1], table[2]]
-        second = [table[0], table[3], table[4]]
-        return jnp.where(
-            leading, jnp.asarray(first, jnp.float32), jnp.asarray(second, jnp.float32)
-        )
-
-    mixing = chosen(inverse_transform)
-    shifts = chosen(diagonal)
-    couple = chosen(coupling)
-    currents = jnp.sum(load_table[:, None, :] * mixing[None], axis=-1)
-    params = jnp.concatenate(
-        [shifts[:2], couple[1:2], jnp.sum(mixing, axis=1), currents.reshape(-1)]
-    )
+    count = 4 * block + 1
+    packs = -(-count // (LANES // margin))
 
     def vmem(*shape):
         return pltpu.VMEM(shape, jnp.float32)
@@ -668,24 +757,28 @@
         return [vmem(count, rows // 2**m + extra, layers, LANES) for m in range(LEVELS)]
 
     mid = rows * margin // LANES if margin < BOTH_CYCLES else 1
-    back = 3 * block * width // LANES
+    groups = block * width // LANES
+    back = max(groups // 2, 1) + 2 * groups
     return pl.pallas_call(
-        functools.partial(kernel, sizes, transform),
+        functools.partial(kernel, sizes, radau_tables()),
         out_shape=(
             jax.ShapeDtypeStruct((SECTIONS, layers, block, wide), jnp.float32),
             jax.ShapeDtypeStruct((layers, block, wide), jnp.float32),
         ),
         in_specs=[
             pl.BlockSpec(memory_space=pltpu.SMEM),
-            pl.BlockSpec(memory_space=pltpu.VMEM),
-            pl.BlockSpec(memory_space=pltpu.VMEM),
+            *[pl.BlockSpec(memory_space=pltpu.VMEM)] * 6,
         ],
         out_specs=(
             pl.BlockSpec(memory_space=pltpu.VMEM),
             pl.BlockSpec(memory_space=pltpu.VMEM),
         ),
         scratch_shapes=[
-            vmem(parts, 4 * block + 1, layers, LANES),
+            vmem(count, layers, wide),
+            vmem(2, packs, layers, LANES),
+            vmem(2, packs, layers, LANES),
+            vmem(regions, count, layers, LANES),
+            vmem(parts, count, layers, LANES),
             vmem(3, parts, block, LANES),
             *levels(8, 0),
             *levels(3, 1),
@@ -694,8 +787,12 @@
             vmem(2, 3, mid, layers, LANES),
             vmem(parts, back, layers, LANES),
             vmem(parts, back, layers, LANES),
-            pltpu.SemaphoreType.DMA((parts,)),
-            pltpu.SemaphoreType.DMA((parts,)),
+            pltpu.SemaphoreType.DMA((2,)),
+            pltpu.SemaphoreType.DMA((2,)),
+            pltpu.SemaphoreType.DMA((regions,)),
+            pltpu.SemaphoreType.DMA((regions,)),
+            pltpu.SemaphoreType.DMA((regions,)),
+            pltpu.SemaphoreType.DMA((regions,)),
             pltpu.SemaphoreType.DMA((2,)),
             pltpu.SemaphoreType.DMA((2,)),
             pltpu.SemaphoreType.DMA((parts,)),
@@ -705,7 +802,7 @@
         compiler_params=pltpu.CompilerParams(
             collective_id=0, has_side_effects=True, vmem_limit_bytes=60 * 1024 * 1024
         ),
-    )(params, send, voltage)
+    )(load_table, voltage, capacity, node_class, via_sites, ball_sites, load_type)
 
 
 def solution(mesh):

time: 96.7 us -> 85.6 us (0.89)
  the two profiles are of different devices: /device:TPU:0 before, /device:TPU:15 now
where the time goes in v1:
time: 85.6 us; the launch traced here: 85.3 us
  Pallas kernels  80.9 us (95%)
  local copies, waits for them, and re-layouts  3.75 us (4%)
    pallas_call x1, Pallas kernels, local(): pl.pallas_call(functools.partial(kernel, sizes, radau_tables()), out_shap...  80.9 us
    unnamed x5, local copies, waits for them, and re-layouts  3.75 us

profile of v1, /device:TPU:15, one launch (start us, length us, event | category | flops | bytes accessed | tf_op | source)
XLA Modules:
  0.0 85.3 jit_solution(1055321754451809131)
XLA Ops:
  0.6 1.4 %copy.9.load_table = f32[16,5]{1,0:T(8,128)} copy(f32[16,5]{0,1:T(8,128)} %param.13) | data formatting | bytes 640 | tf_op args[6]
  2.0 80.9 %shard_map.86 = (f32[5,8,8,256]{3,2,1,0:T(8,128)}, f32[8,8,256]{2,1,0:T(8,128)}) custom-call(f32[16,5]{1,0:T(8,128)} %copy.9.load_table, f32[8,8,256]{2,1,0:T(8,128)} %voltage.1, f32[8,8,256]{2,1,0:T(8,128)} %capacity.1, s32[8,8,256]{2,1,0:T(8,128)} %node_class.1, s32[7,8,256]{2,1,0:T(8,128)} %via_sites.1, s32[8,256]{1,0:T(8,128)} %ball_sites.1, ...), custom_call_target="tpu_custom_call" | custom-call | tf_op jit(solution)/shard_map/pallas_call | solution.py:762
  82.9 0.0 copy-start
  82.9 1.8 %copy.12 = f32[5,8,8,256]{3,2,1,0:T(8,128)} copy(f32[5,8,8,256]{3,2,1,0:T(8,128)} %get-tuple-element.4) | data formatting | bytes 655360
  84.7 0.0 copy-done
  84.7 0.6 copy.13
Async XLA Ops:
  82.9 1.8 %copy-start = (f32[8,8,256]{2,1,0:T(8,128)S(1)}, f32[8,8,256]{2,1,0:T(8,128)}, u32[]{:S(2)}) copy-start(f32[8,8,256]{2,1,0:T(8,128)} %get-tuple-element.5) | copy-start | bytes 196612

commit v2 on v1

--- a/solution.py
+++ b/solution.py
@@ -213,14 +213,14 @@
     return lax.broadcasted_iota(jnp.int32, (layers, LANES), 0)
 
 
-def flux(here, ahead, behind_flux, gx, gy, gv, stride):
+def flux(here, ahead, behind_flux, gx, gy, gv, stride, gy_low=None, gv_low=None):
+    if gy_low is None:
+        gy_low, gv_low = right_by(gy, stride), from_below(gv)
     along_x = gx * (ahead - here)
-    along_y = gy * (left_by(here, stride) - here)
-    along_z = gv * (from_above(here) - here)
     total = (
         (along_x - behind_flux)
-        + (along_y - right_by(along_y, stride))
-        + (along_z - from_below(along_z))
+        + (gy * (left_by(here, stride) - here) + gy_low * (right_by(here, stride) - here))
+        + (gv * (from_above(here) - here) + gv_low * (from_below(here) - here))
     )
     return along_x, total
 
@@ -251,7 +251,7 @@
     rows = g.shape[1]
     layers = g.shape[2]
     stride = 2**level
-    step = min(4, rows)
+    step = min(16, rows)
     zero = jnp.zeros((layers, LANES), jnp.float32)
 
     def value(k, base, half, r):
@@ -273,12 +273,13 @@
             i = base + r
             gx, gy, gv = g[0, i], g[1, i], g[2, i]
             ground, cap = g[3, i], g[4, i]
+            gy_low, gv_low = g[8, i], g[9, i]
             local = (lam0 * cap + ground, alpha * cap + ground)
             mate = beta * cap
             x0, x1, x2 = xs[0][r], xs[1][r], xs[2][r]
             pulled = []
             for k in range(3):
-                behind[k], total = flux(xs[k][r], xs[k][r + 1], behind[k], gx, gy, gv, stride)
+                behind[k], total = flux(xs[k][r], xs[k][r + 1], behind[k], gx, gy, gv, stride, gy_low, gv_low)
                 pulled.append(total)
             residual = (
                 f_ref[0, i] - local[0] * x0 + pulled[0],
@@ -334,7 +335,8 @@
             cap = group_lanes(g[4, j] + g[4, j + 1], stride, low_half)
             total = gx + behind + gy + right_by(gy, 2 * stride) + gv + from_below(gv) + ground
             found = weights(cap, total, *scal)
-            for k, entry in enumerate((gx, gy, gv, ground, cap) + found):
+            lows = (right_by(gy, 2 * stride), from_below(gv))
+            for k, entry in enumerate((gx, gy, gv, ground, cap) + found + lows):
                 g_next[k, i] = entry
             behind = gx
         return behind
@@ -593,7 +595,8 @@
             found = weights(cap, total, *scal)
             behind_flux, pulled = flux(volt, volt_ahead, behind_flux, gx, gy, gv, 1)
             leak = ground * volt - pulled
-            for k, entry in enumerate((gx, gy, gv, ground, cap) + found):
+            lows = (right_by(gy, 1), from_below(gv))
+            for k, entry in enumerate((gx, gy, gv, ground, cap) + found + lows):
                 g0[k, i] = entry
             source = [
                 jnp.where(
@@ -780,7 +783,7 @@
             vmem(regions, count, layers, LANES),
             vmem(parts, count, layers, LANES),
             vmem(3, parts, block, LANES),
-            *levels(8, 0),
+            *levels(10, 0),
             *levels(3, 1),
             *levels(3, 0),
             vmem(2, 3, mid, layers, LANES),

time: 85.6 us -> 57 us (0.67)
  Pallas kernels: 80.9 us -> 52.4 us
    pallas_call x1, Pallas kernels: 80.9 us -> 52.4 us  [local(): pl.pallas_call(functools.partial(kernel, sizes, radau_tables()), out_shap...]
where the time goes in v2:
time: 57 us; the launch traced here: 56.8 us
  Pallas kernels  52.4 us (92%)
  local copies, waits for them, and re-layouts  3.75 us (7%)
  between operations  0.65 us (1%)
    pallas_call x1, Pallas kernels, local(): pl.pallas_call(functools.partial(kernel, sizes, radau_tables()), out_shap...  52.4 us
    unnamed x5, local copies, waits for them, and re-layouts  3.75 us

profile of v2, /device:TPU:15, one launch (start us, length us, event | category | flops | bytes accessed | tf_op | source)
XLA Modules:
  0.0 56.8 jit_solution(11420929721318544782)
XLA Ops:
  0.6 1.4 %copy.9.load_table = f32[16,5]{1,0:T(8,128)} copy(f32[16,5]{0,1:T(8,128)} %param.13) | data formatting | bytes 640 | tf_op args[6]
  2.0 52.4 %shard_map.86 = (f32[5,8,8,256]{3,2,1,0:T(8,128)}, f32[8,8,256]{2,1,0:T(8,128)}) custom-call(f32[16,5]{1,0:T(8,128)} %copy.9.load_table, f32[8,8,256]{2,1,0:T(8,128)} %voltage.1, f32[8,8,256]{2,1,0:T(8,128)} %capacity.1, s32[8,8,256]{2,1,0:T(8,128)} %node_class.1, s32[7,8,256]{2,1,0:T(8,128)} %via_sites.1, s32[8,256]{1,0:T(8,128)} %ball_sites.1, ...), custom_call_target="tpu_custom_call" | custom-call | tf_op jit(solution)/shard_map/pallas_call | solution.py:765
  54.4 0.0 copy-start
  54.4 1.8 %copy.12 = f32[5,8,8,256]{3,2,1,0:T(8,128)} copy(f32[5,8,8,256]{3,2,1,0:T(8,128)} %get-tuple-element.4) | data formatting | bytes 655360
  56.1 0.0 copy-done
  56.1 0.6 %copy.13 = f32[8,8,256]{2,1,0:T(8,128)} copy(f32[8,8,256]{2,1,0:T(8,128)S(1)} %copy-done) | data formatting | bytes 131072
Async XLA Ops:
  54.4 1.8 %copy-start = (f32[8,8,256]{2,1,0:T(8,128)S(1)}, f32[8,8,256]{2,1,0:T(8,128)}, u32[]{:S(2)}) copy-start(f32[8,8,256]{2,1,0:T(8,128)} %get-tuple-element.5) | copy-start | bytes 196612
